TPU v7x, 32 devices: a whole 2x2x4 slice. The times are simulated.
32 devices in a mesh: grp: 2 (over y), frm: 4 (over z), row: 4 (over x, core).
Axes of the slice: x: 2, y: 2, z: 4, core: 2. Of those that a mesh axis runs over, the one named last changes fastest.
Arguments:
- hidden_in: bfloat16 [512, 16, 2240], P('row', ('grp', 'frm')), parts along dimension 1, may hold values from -6 to 6
- norm_gain: float32 [2240], replicated, may hold values from 0.1 to 1.9
- query_key_value_weight: bfloat16 [2240, 3, 2240], P(None, None, 'row'), may hold values from -0.125 to 0.125
- head_gain: float32 [2240], P('row'), may hold values from 0.1 to 1.9
- output_matrix: bfloat16 [2240, 2240], P('row'), may hold values from -0.125 to 0.125
- block_end: int32 [16], P(('grp', 'frm')), parts along dimension 0, may hold values from 0 to 7, as said below
Outputs:
- mixed_out: bfloat16 [512, 16, 2240], P('row', ('grp', 'frm')), parts along dimension 1
There are 2 independent parts, one for each index of `grp`. A program takes and returns all parts, laid end to end along the dimension named above; an argument that names none is the same for every part. Nothing has to cross between parts.
Inputs may be any that keep to these rules, and one draw needn't show every extreme that they name: `block_end`: entries never fall from one frame to the next; each entry is at least its frame's index, and frames with equal entries form a block of consecutive frames; a block never holds frames of two different runs of 2 frames (f // 2 differs), and the last frame of every such run ends a block.
All inputs are finite; a program needn't handle non-finite values.
Results may differ from a plain program's by a relative error of at most 0.015.
Values may be sent and summed in bfloat16 or wider, within the bound.
No kernel may reach another device: no remote copies, remote signals or barrier semaphores. Data moves between devices by JAX's collectives and lax.ppermute only.
A program may use at most 64 MiB of HBM per device.

v0:
```python
import jax
import jax.numpy as jnp
from jax import lax
from jax.sharding import PartitionSpec as P

HD = 112
epsilon = 1e-06


def per_device(hidden_in, norm_gain, query_key_value_weight, head_gain, output_matrix, block_end):
    slab_rows, own_frames, model_width = hidden_in.shape
    local_heads = head_gain.shape[0] // HD
    group_width = local_heads * HD
    as_float = hidden_in.astype(jnp.float32)
    mean_square = jnp.mean(as_float * as_float, axis=-1, keepdims=True)
    normed = (as_float * lax.rsqrt(mean_square + epsilon) * norm_gain).astype(jnp.bfloat16)
    weights = query_key_value_weight.reshape(model_width, 3 * group_width)
    rows_per_block = lax.all_gather(normed, "row", axis=0, tiled=True)
    flat = rows_per_block.reshape(-1, model_width)
    result = jnp.dot(flat, weights, preferred_element_type=jnp.float32).astype(jnp.bfloat16)
    projected = result.reshape(rows_per_block.shape[0], own_frames, 3 * group_width)
    projected = projected.reshape(-1, own_frames, 3, local_heads, HD)
    queries = jax.nn.relu(projected[:, :, 0])
    key_relu = jax.nn.relu(projected[:, :, 1])
    values = projected[:, :, 2]
    per_frame_state = jnp.einsum(
        "pfhi,pfhj->fhij", key_relu, values, preferred_element_type=jnp.float32
    )
    per_device_sum = jnp.sum(per_frame_state, axis=0)
    earlier_mask = (block_end[None, :] <= block_end[:, None]).astype(jnp.float32)
    inside = jnp.einsum(
        "fg,ghij->fhij", earlier_mask, per_frame_state, precision=lax.Precision.HIGHEST
    )
    my_index = lax.axis_index("frm")
    rows_per_block = lax.all_gather(
        per_device_sum[None].astype(jnp.bfloat16), "frm", axis=0, tiled=True
    ).astype(jnp.float32)
    owners = jnp.arange(rows_per_block.shape[0], dtype=jnp.int32)
    include = (owners < my_index).astype(jnp.float32)
    prior_frames_sum = jnp.zeros_like(per_device_sum) + jnp.einsum(
        "n,nhij->hij", include, rows_per_block, precision=lax.Precision.HIGHEST
    )
    block_state = (inside + prior_frames_sum[None]).astype(jnp.bfloat16)
    attended = jnp.einsum(
        "pfhi,fhij->pfhj", queries, block_state, preferred_element_type=jnp.float32
    )
    head_square = jnp.mean(attended * attended, axis=-1, keepdims=True)
    head_out = (
        attended * lax.rsqrt(head_square + epsilon) * head_gain.reshape(local_heads, HD)
    ).astype(jnp.bfloat16)
    merged_heads = head_out.reshape(head_out.shape[0], own_frames, group_width)
    own_tokens = lax.all_to_all(merged_heads, "row", split_axis=0, concat_axis=2, tiled=True)
    rows_per_block = lax.all_gather(output_matrix, "row", axis=0, tiled=True)
    shards = rows_per_block.shape[0] // group_width
    split_cols = own_tokens.reshape(slab_rows, own_frames, shards, group_width)
    split_rows = rows_per_block.reshape(shards, group_width, model_width)
    products = jnp.einsum(
        "pfkc,kcd->kpfd", split_cols, split_rows, preferred_element_type=jnp.float32
    )
    rounded = lax.optimization_barrier(products.astype(jnp.bfloat16)).astype(jnp.float32)
    summed = jnp.sum(rounded, axis=0)
    return summed.astype(jnp.bfloat16)


def solution(mesh):
    placed = (
        P("row", ("grp", "frm"), None),
        P(),
        P(None, None, "row"),
        P("row"),
        P("row", None),
        P(("grp", "frm")),
    )
    return jax.shard_map(
        per_device,
        mesh=mesh,
        in_specs=placed,
        out_specs=P("row", ("grp", "frm"), None),
        check_vma=False,
    )
```

profile of v0, /device:TPU:0, one launch (start us, length us, event | category | flops | bytes accessed | tf_op | source)
XLA Modules:
  0.0 184.6 jit_solution(13249381109375235139)
XLA Ops:
  6.5 0.0 all-gather.4.cloned.1.call-start
  6.5 1.6 fusion
  8.1 2.6 %fusion.2 = bf16[128,2,2240]{0,2,1:T(8,128)(2,1)} fusion(bf16[128,2,2240]{0,2,1:T(8,128)(2,1)} %param.6, f32[2240]{0:T(1024)} %param.7, f32[128,2]{0,1:T(2,128)S(1)} %add_rsqrt_fusion.1), kind=kLoop, calls=%fused_computation.6 | loop fusion | flops 2293760 | bytes 2303744 | tf_op jit(solution)/shard_map/convert_element_type | solution.py:16
  10.8 0.0 all-gather.4.cloned.1.call-update
  10.8 0.0 all-gather.6.cloned.1.call-start
  10.8 0.7 all-gather.6.cloned.1.call-update
  11.5 0.0 copy-done
  11.6 0.1 mul.48
  11.6 39.3 %all-gather.4.cloned.1.call-done = bf16[512,2,2240]{0,2,1:T(8,128)(2,1)} async-done(((bf16[128,2,2240]{0,2,1:T(8,128)(2,1)}), bf16[512,2,2240]{0,2,1:T(8,128)(2,1)}) %all-gather.4.cloned.1.call-update) | async-done | bytes 4587536 | tf_op jit(solution)/shard_map/all_gather | solution.py:18
  50.9 12.8 %copy.16 = bf16[512,2,2240]{2,1,0:T(2,128)(2,1)} copy(bf16[512,2,2240]{0,2,1:T(8,128)(2,1)} %all-gather.4.cloned.1.call-done) | data formatting | bytes 9175040 | tf_op jit(solution)/shard_map/all_gather | solution.py:18
  63.8 10.8 %reshape.48 = bf16[1024,2240]{1,0:T(8,128)(2,1)} reshape(bf16[512,2,2240]{2,1,0:T(2,128)(2,1)} %copy.16) | data formatting | bytes 9175040 | tf_op jit(solution)/shard_map/reshape | solution.py:19
  74.5 11.9 %convolution_convert_fusion.1 = bf16[1024,1680]{0,1:T(8,128)(2,1)S(1)} fusion(bf16[1024,2240]{1,0:T(8,128)(2,1)} %reshape.48, bf16[2240,1680]{0,1:T(8,128)(2,1)} %bitcast.55), kind=kOutput, calls=%fused_computation.1 | convolution fusion | flops 7708753920 | bytes 15554560 | tf_op jit(solution)/shard_map/dot_general | solution.py:20
  86.5 3.8 %copy.17 = bf16[1024,1680]{1,0:T(8,128)(2,1)} copy(bf16[1024,1680]{0,1:T(8,128)(2,1)S(1)} %convolution_convert_fusion.1) | data formatting | bytes 6881280 | tf_op jit(solution)/shard_map/convert_element_type | solution.py:20
  90.2 11.4 %reshape_reshape.3 = bf16[512,2,3,5,112]{4,3,2,1,0:T(8,128)(2,1)} reshape(bf16[1024,1680]{1,0:T(8,128)(2,1)} %copy.17) | data formatting | bytes 6881280 | tf_op jit(solution)/shard_map/reshape;reshape | solution.py:22
  101.7 5.9 %fusion.29 = (bf16[512,2,1,5,112]{4,3,2,1,0:T(8,128)(2,1)}, bf16[512,2,1,5,112]{4,3,2,1,0:T(8,128)(2,1)}, bf16[512,2,1,5,112]{4,3,2,1,0:T(8,128)(2,1)S(1)}) fusion(bf16[512,2,3,5,112]{4,3,2,1,0:T(8,128)(2,1)} %reshape_reshape.3), kind=kLoop, calls=%fused_computation.39 | loop fusion | bytes 6881280 | tf_op jit(solution)/shard_map/slice | solution.py:24
  107.6 4.1 %copy.33 = bf16[512,2,1,5,112]{0,4,3,1,2:T(8,128)(2,1)} copy(bf16[512,2,1,5,112]{4,3,2,1,0:T(8,128)(2,1)} %get-tuple-element.5) | data formatting | bytes 2293760
  111.6 4.1 %copy.34 = bf16[512,2,1,5,112]{0,4,3,1,2:T(8,128)(2,1)} copy(bf16[512,2,1,5,112]{4,3,2,1,0:T(8,128)(2,1)} %get-tuple-element.6) | data formatting | bytes 2293760
  115.7 1.4 copy.35
  117.1 0.0 copy-start.1
  117.1 2.1 %fusion.30 = (bf16[5,112,112]{2,1,0:T(8,128)(2,1)S(1)}, f32[2,5,112,112]{3,2,1,0:T(8,128)S(1)}) fusion(bf16[512,2,1,5,112]{0,4,3,1,2:T(8,128)(2,1)} %copy.34, bf16[512,2,1,5,112]{0,4,3,1,2:T(8,128)(2,1)} %copy.33), kind=kOutput, calls=%fused_computation.40 | convolution fusion | flops 129086720 | bytes 2920960 | tf_op jit(solution)/shard_map/pfhi,pfhj->fhij/dot_general | solution.py:26
  119.2 17.1 %all-gather = bf16[20,112,112]{2,1,0:T(8,128)(2,1)S(1)} all-gather(bf16[5,112,112]{2,1,0:T(8,128)(2,1)S(1)} %get-tuple-element.8), channel_id=2, replica_groups=mesh['grp'=2,'frm'=4,'row'=4] {'frm'}, dimensions={0}, use_global_device_ids=true | all-gather | bytes 627200 | tf_op jit(solution)/shard_map/all_gather | solution.py:35
  136.3 0.4 fusion.18
  136.7 0.0 copy-done.1
  136.7 1.5 fusion.6
  138.2 0.5 fusion.3
  138.8 0.3 fusion.5
  139.1 1.9 %copy.23 = bf16[512,2,560]{2,1,0:T(2,128)(2,1)S(1)} copy(bf16[512,2,560]{0,2,1:T(8,128)(2,1)S(1)} %bitcast.52) | data formatting | bytes 2293760 | tf_op jit(solution)/shard_map/reshape | solution.py:51
  141.0 19.7 %all_to_all.15 = bf16[512,2,560]{2,1,0:T(2,128)(2,1)S(1)} all-to-all(bf16[512,2,560]{2,1,0:T(2,128)(2,1)S(1)} %copy.23), channel_id=1, replica_groups=mesh['grp'=2,'frm'=4,'row'=4] {'row'}, dimensions={0} | all-to-all | bytes 2293760 | tf_op jit(solution)/shard_map/all_to_all | solution.py:52
  160.7 2.0 %copy.25 = bf16[4,128,2,560]{1,3,2,0:T(8,128)(2,1)S(1)} copy(bf16[4,128,2,560]{3,2,1,0:T(2,128)(2,1)S(1)} %bitcast.51) | data formatting | bytes 2293760 | tf_op jit(solution)/shard_map/all_to_all | solution.py:52
  162.7 0.0 all-gather.6.cloned.1.call-done
  162.7 10.8 %convolution_convert_fusion = bf16[4,128,2,2240]{1,3,2,0:T(8,128)(2,1)} fusion(bf16[4,560,2240,1]{2,1,3,0:T(8,128)(2,1)} %bitcast.54, bf16[4,128,2,560]{1,3,2,0:T(8,128)(2,1)S(1)} %copy.25), kind=kOutput, calls=%fused_computation | convolution fusion | flops 2571304960 | bytes 15769600 | tf_op jit(solution)/shard_map/pfkc,kcd->kpfd/dot_general | solution.py:57
  173.5 4.3 %reduce_sum.42 = bf16[128,2,2240]{0,2,1:T(8,128)(2,1)} reduce(bf16[4,128,2,2240]{1,3,2,0:T(8,128)(2,1)} %convolution_convert_fusion, bf16[]{:T(256)} %constant.17.clone.1), dimensions={0}, to_apply=%region_3.4 | reduce | flops 1720320 | bytes 5734402 | tf_op jit(solution)/shard_map/reduce_sum | solution.py:61
  (3 shorter events, 0.0 us)
Async XLA Ops:
  6.5 44.4 %all-gather.4.cloned.1.call-start = ((), (), s32[]{:S(2)}) async-start(), calls=%async_computation.1 | async-start | bytes 5734400 | tf_op jit(solution)/shard_map/all_gather | solution.py:18
  10.8 0.8 copy-start
  10.8 151.9 %all-gather.6.cloned.1.call-start = ((), (), s32[]{:S(2)}) async-start(), calls=%async_computation.2 | async-start | bytes 12902400 | tf_op jit(solution)/shard_map/all_gather | solution.py:53
  117.1 19.6 %copy-start.1 = (s32[2]{0:T(128)S(1)}, s32[2]{0:T(128)}, u32[]{:S(2)}) copy-start(s32[2]{0:T(128)} %param.11) | copy-start | bytes 28
Sparse Core Ops, SparseCore 0:
  10.9 39.9 all-gather.3
  52.5 69.2 all-gather.5
where the time goes:
time: 186 us; the launch traced here: 185 us
  local copies, waits for them, and re-layouts  58.2 us (31%)
  waiting for transfers between devices  40.1 us (22%)
  blocking collectives  36.8 us (20%)
  matrix products  27.2 us (15%)
  between operations  13.5 us (7%)
  other arithmetic  8.82 us (5%)
    all_gather x1, waiting for transfers between devices, per_device(): rows_per_block = lax.all_gather(normed, 'row', axis=0, tiled=True)  39.3 us
    all_to_all x1, blocking collectives, per_device(): lax.all_to_all(merged_heads, 'row', split_axis=0, concat_axis=2, tiled=True)  19.7 us
    all_gather x1, blocking collectives, per_device(): lax.all_gather(per_device_sum[None].astype(jnp.bfloat16), 'frm', axis=0,...  17.1 us
    all_gather x1, local copies, waits for them, and re-layouts, per_device(): rows_per_block = lax.all_gather(normed, 'row', axis=0, tiled=True)  12.8 us
    dot_general x1, matrix products, per_device(): jnp.dot(flat, weights, preferred_element_type=jnp.float32)  11.9 us
    another operation x1, local copies, waits for them, and re-layouts, per_device(): projected = projected.reshape(-1, own_frames, 3, local_heads, HD)  11.4 us
    dot_general x1, matrix products, per_device(): jnp.einsum('pfkc,kcd->kpfd', split_cols, split_rows, preferred_element_ty...  10.8 us
    reshape x1, local copies, waits for them, and re-layouts, per_device(): flat = rows_per_block.reshape(-1, model_width)  10.8 us
  transfers between devices with their start and end apart: 2, of which 1 were waited for; matrix products, arithmetic and copies ran while one was open for 41% of the time, Pallas kernels for 0%

commit v1 on v0

--- a/solution.py
+++ b/solution.py
@@ -5,6 +5,12 @@
 
 HD = 112
 epsilon = 1e-06
+
+
+def swap_blocks(shard, axis, split, join):
+    pieces = jnp.split(shard, lax.axis_size(axis), axis=split)
+    incoming = lax.all_to_all(jnp.stack(pieces), axis, 0, 0)
+    return jnp.concatenate(incoming, axis=join)
 
 
 def per_device(hidden_in, norm_gain, query_key_value_weight, head_gain, output_matrix, block_end):
@@ -49,7 +55,7 @@
         attended * lax.rsqrt(head_square + epsilon) * head_gain.reshape(local_heads, HD)
     ).astype(jnp.bfloat16)
     merged_heads = head_out.reshape(head_out.shape[0], own_frames, group_width)
-    own_tokens = lax.all_to_all(merged_heads, "row", split_axis=0, concat_axis=2, tiled=True)
+    own_tokens = swap_blocks(merged_heads, "row", 0, 2)
     rows_per_block = lax.all_gather(output_matrix, "row", axis=0, tiled=True)
     shards = rows_per_block.shape[0] // group_width
     split_cols = own_tokens.reshape(slab_rows, own_frames, shards, group_width)

time: 186 us -> 180 us (0.968)
  local copies, waits for them, and re-layouts: 58.2 us -> 54.5 us
  blocking collectives: 36.8 us -> 34.8 us
    all_to_all x1 -> x0, local copies, waits for them, and re-layouts: 1.97 us -> none  [per_device(): lax.all_to_all(merged_heads, 'row', split_axis=0, concat_axis=2, tiled=True)]
    reshape x1 -> x0, local copies, waits for them, and re-layouts: 1.94 us -> none  [per_device(): merged_heads = head_out.reshape(head_out.shape[0], own_frames, group_width)]
  transfers between devices with their start and end apart: 2 -> 2, of which waited for: 1 -> 1; matrix products, arithmetic and copies ran while one was open for 41% -> 40% of each run, Pallas kernels for 0% -> 0%
where the time goes in v1:
time: 180 us; the launch traced here: 179 us
  local copies, waits for them, and re-layouts  54.5 us (30%)
  waiting for transfers between devices  40 us (22%)
  blocking collectives  34.8 us (19%)
  matrix products  27.2 us (15%)
  between operations  13.5 us (8%)
  other arithmetic  8.96 us (5%)
    all_gather x1, waiting for transfers between devices, per_device(): rows_per_block = lax.all_gather(normed, 'row', axis=0, tiled=True)  39.3 us
    all_to_all x1, blocking collectives, swap_blocks(): incoming = lax.all_to_all(jnp.stack(pieces), axis, 0, 0)  17.9 us
    all_gather x1, blocking collectives, per_device(): lax.all_gather(per_device_sum[None].astype(jnp.bfloat16), 'frm', axis=0,...  16.9 us
    all_gather x1, local copies, waits for them, and re-layouts, per_device(): rows_per_block = lax.all_gather(normed, 'row', axis=0, tiled=True)  12.8 us
    dot_general x1, matrix products, per_device(): jnp.dot(flat, weights, preferred_element_type=jnp.float32)  11.9 us
    another operation x1, local copies, waits for them, and re-layouts, per_device(): projected = projected.reshape(-1, own_frames, 3, local_heads, HD)  11.4 us
    dot_general x1, matrix products, per_device(): jnp.einsum('pfkc,kcd->kpfd', split_cols, split_rows, preferred_element_ty...  10.8 us
    reshape x1, local copies, waits for them, and re-layouts, per_device(): flat = rows_per_block.reshape(-1, model_width)  10.8 us
  transfers between devices with their start and end apart: 2, of which 1 were waited for; matrix products, arithmetic and copies ran while one was open for 40% of the time, Pallas kernels for 0%

profile of v1, /device:TPU:0, one launch (start us, length us, event | category | flops | bytes accessed | tf_op | source)
XLA Modules:
  0.0 179.1 jit_solution(15093926075854131767)
XLA Ops:
  6.5 0.0 all-gather.4.cloned.1.call-start
  6.5 1.6 fusion
  8.1 2.6 %fusion.2 = bf16[128,2,2240]{0,2,1:T(8,128)(2,1)} fusion(bf16[128,2,2240]{0,2,1:T(8,128)(2,1)} %param.6, f32[2240]{0:T(1024)} %param.7, f32[128,2]{0,1:T(2,128)S(1)} %add_rsqrt_fusion.1), kind=kLoop, calls=%fused_computation.6 | loop fusion | flops 2293760 | bytes 2303744 | tf_op jit(solution)/shard_map/convert_element_type | solution.py:22
  10.8 0.0 copy-start
  10.8 0.0 all-gather.4.cloned.1.call-update
  10.8 0.0 all-gather.6.cloned.1.call-start
  10.8 0.7 all-gather.6.cloned.1.call-update
  11.5 0.0 copy-done
  11.6 0.1 mul.48
  11.6 39.3 %all-gather.4.cloned.1.call-done = bf16[512,2,2240]{0,2,1:T(8,128)(2,1)} async-done(((bf16[128,2,2240]{0,2,1:T(8,128)(2,1)}), bf16[512,2,2240]{0,2,1:T(8,128)(2,1)}) %all-gather.4.cloned.1.call-update) | async-done | bytes 4587536 | tf_op jit(solution)/shard_map/all_gather | solution.py:24
  50.9 12.8 %copy.15 = bf16[512,2,2240]{2,1,0:T(2,128)(2,1)} copy(bf16[512,2,2240]{0,2,1:T(8,128)(2,1)} %all-gather.4.cloned.1.call-done) | data formatting | bytes 9175040 | tf_op jit(solution)/shard_map/all_gather | solution.py:24
  63.8 10.8 %reshape.55 = bf16[1024,2240]{1,0:T(8,128)(2,1)} reshape(bf16[512,2,2240]{2,1,0:T(2,128)(2,1)} %copy.15) | data formatting | bytes 9175040 | tf_op jit(solution)/shard_map/reshape | solution.py:25
  74.5 11.9 %convolution_convert_fusion.1 = bf16[1024,1680]{0,1:T(8,128)(2,1)S(1)} fusion(bf16[1024,2240]{1,0:T(8,128)(2,1)} %reshape.55, bf16[2240,1680]{0,1:T(8,128)(2,1)} %bitcast.59), kind=kOutput, calls=%fused_computation.1 | convolution fusion | flops 7708753920 | bytes 15554560 | tf_op jit(solution)/shard_map/dot_general | solution.py:26
  86.5 3.7 %copy.16 = bf16[1024,1680]{1,0:T(8,128)(2,1)} copy(bf16[1024,1680]{0,1:T(8,128)(2,1)S(1)} %convolution_convert_fusion.1) | data formatting | bytes 6881280 | tf_op jit(solution)/shard_map/convert_element_type | solution.py:26
  90.2 11.4 %reshape_reshape.3 = bf16[512,2,3,5,112]{4,3,2,1,0:T(8,128)(2,1)} reshape(bf16[1024,1680]{1,0:T(8,128)(2,1)} %copy.16) | data formatting | bytes 6881280 | tf_op jit(solution)/shard_map/reshape;reshape | solution.py:28
  101.6 5.9 %fusion.29 = (bf16[512,2,1,5,112]{4,3,2,1,0:T(8,128)(2,1)}, bf16[512,2,1,5,112]{4,3,2,1,0:T(8,128)(2,1)}, bf16[512,2,1,5,112]{4,3,2,1,0:T(8,128)(2,1)S(1)}) fusion(bf16[512,2,3,5,112]{4,3,2,1,0:T(8,128)(2,1)} %reshape_reshape.3), kind=kLoop, calls=%fused_computation.40 | loop fusion | bytes 6881280 | tf_op jit(solution)/shard_map/slice | solution.py:30
  107.6 4.1 %copy.27 = bf16[512,2,1,5,112]{0,4,3,1,2:T(8,128)(2,1)} copy(bf16[512,2,1,5,112]{4,3,2,1,0:T(8,128)(2,1)} %get-tuple-element.5) | data formatting | bytes 2293760
  111.6 4.1 %copy.28 = bf16[512,2,1,5,112]{0,4,3,1,2:T(8,128)(2,1)} copy(bf16[512,2,1,5,112]{4,3,2,1,0:T(8,128)(2,1)} %get-tuple-element.6) | data formatting | bytes 2293760
  115.7 1.4 copy.29
  117.1 0.0 copy-start.1
  117.1 2.1 %fusion.31 = (bf16[5,112,112]{2,1,0:T(8,128)(2,1)S(1)}, f32[2,5,112,112]{3,2,1,0:T(8,128)S(1)}) fusion(bf16[512,2,1,5,112]{0,4,3,1,2:T(8,128)(2,1)} %copy.28, bf16[512,2,1,5,112]{0,4,3,1,2:T(8,128)(2,1)} %copy.27), kind=kOutput, calls=%fused_computation.42 | convolution fusion | flops 129086720 | bytes 2920960 | tf_op jit(solution)/shard_map/pfhi,pfhj->fhij/dot_general | solution.py:32
  119.2 16.9 %all-gather = bf16[20,112,112]{2,1,0:T(8,128)(2,1)S(1)} all-gather(bf16[5,112,112]{2,1,0:T(8,128)(2,1)S(1)} %get-tuple-element.12), channel_id=2, replica_groups=mesh['grp'=2,'frm'=4,'row'=4] {'frm'}, dimensions={0}, use_global_device_ids=true | all-gather | bytes 627200 | tf_op jit(solution)/shard_map/all_gather | solution.py:41
  136.1 0.4 fusion.18
  136.5 0.0 copy-done.1
  136.6 1.5 fusion.6
  138.0 0.5 fusion.3
  138.6 0.3 fusion.5
  138.9 0.2 fusion.30
  139.1 0.1 pad_maximum_fusion
  139.2 17.9 %all_to_all.5 = bf16[4,128,2,560]{1,3,2,0:T(8,128)(2,1)S(1)} all-to-all(bf16[4,128,2,560]{1,3,2,0:T(8,128)(2,1)S(1)} %pad_maximum_fusion), channel_id=1, replica_groups=mesh['grp'=2,'frm'=4,'row'=4] {'row'}, dimensions={0} | all-to-all | bytes 2293760 | tf_op jit(solution)/shard_map/all_to_all | solution.py:12
  157.1 10.8 %convolution_convert_fusion = bf16[4,128,2,2240]{1,3,2,0:T(8,128)(2,1)} fusion(bf16[4,560,2240,1]{2,1,3,0:T(8,128)(2,1)} %bitcast.58, bf16[4,128,2,560]{1,3,2,0:T(8,128)(2,1)S(1)} %all_to_all.5), kind=kOutput, calls=%fused_computation | convolution fusion | flops 2571304960 | bytes 15769600 | tf_op jit(solution)/shard_map/pfkc,kcd->kpfd/dot_general | solution.py:63
  167.9 4.3 %reduce_sum.42 = bf16[128,2,2240]{0,2,1:T(8,128)(2,1)} reduce(bf16[4,128,2,2240]{1,3,2,0:T(8,128)(2,1)} %convolution_convert_fusion, bf16[]{:T(256)} %constant.17.clone.1), dimensions={0}, to_apply=%region_3.4 | reduce | flops 1720320 | bytes 5734402 | tf_op jit(solution)/shard_map/reduce_sum | solution.py:67
  (3 shorter events, 0.0 us)
Async XLA Ops:
  6.5 44.4 %all-gather.4.cloned.1.call-start = ((), (), s32[]{:S(2)}) async-start(), calls=%async_computation.1 | async-start | bytes 5734400 | tf_op jit(solution)/shard_map/all_gather | solution.py:24
  10.8 0.8 copy-start
  10.8 146.4 %all-gather.6.cloned.1.call-start = ((), (), s32[]{:S(2)}) async-start(), calls=%async_computation.2 | async-start | bytes 12902400 | tf_op jit(solution)/shard_map/all_gather | solution.py:59
  117.1 19.5 %copy-start.1 = (s32[2]{0:T(128)S(1)}, s32[2]{0:T(128)}, u32[]{:S(2)}) copy-start(s32[2]{0:T(128)} %param.11) | copy-start | bytes 28
Sparse Core Ops, SparseCore 0:
  10.9 39.9 all-gather.3
  52.5 69.2 all-gather.5
